TPU v7x, 32 devices: a whole 2x2x4 slice. The times are simulated.
32 devices in a mesh: dp: 8 (over y, x, core), tensor: 4 (over z).
Axes of the slice: x: 2, y: 2, z: 4, core: 2. Of those that a mesh axis runs over, the one named last changes fastest.
Arguments:
- rm_hidden: bfloat16 [8, 256, 3584], P('dp', 'tensor'), may hold values from -6 to 6
- rm_cotangent: bfloat16 [8, 256, 3584], P('dp', 'tensor'), may hold values from -6 to 6
- rm_gain: float32 [3584], replicated, may hold values from 0.25 to 1.75
- rewards: float32 [8], P('dp'), may hold values from 0.25 to 8, as said below
- visual_pos: int32 [8, 128], P('dp', 'tensor'), may hold values from 0 to 255, as said below
- bridge: bfloat16 [3584, 2048], P(None, 'tensor'), may hold values from -0.09375 to 0.09375
- img_query: bfloat16 [8, 512, 2048], P('dp', 'tensor'), may hold values from -8 to 8
- img_key: bfloat16 [8, 512, 2048], P('dp', 'tensor'), may hold values from -8 to 8
- img_value: bfloat16 [8, 512, 2048], P('dp', 'tensor'), may hold values from -6 to 6
Outputs:
- grad_query: bfloat16 [8, 512, 2048], P('dp', 'tensor')
- grad_key: bfloat16 [8, 512, 2048], P('dp', 'tensor')
- grad_value: bfloat16 [8, 512, 2048], P('dp', 'tensor')
Inputs may be any that keep to these rules, and one draw needn't show every extreme that they name: `visual_pos`: strictly increasing in each sample; rows 64 * t to 64 * t + 63 of a reward sequence hold exactly 32 visual tokens, for every t. `rewards`: positive.
All inputs are finite; a program needn't handle non-finite values.
Results may differ from a plain program's by a relative error of at most 0.0082.
Values may be sent and summed in bfloat16 or wider, within the bound.
No kernel may reach another device: no remote copies, remote signals or barrier semaphores. Data moves between devices by JAX's collectives and lax.ppermute only.
A program may use at most 64 MiB of HBM per device.

v0:
```python
import jax
import jax.numpy as jnp
from jax import lax
from jax.sharding import PartitionSpec as P

HD = 128
GW = 64


def norm_backward(hidden, cotangent, gain):
    hidden_f = hidden.astype(jnp.float32)
    scaled_cot = cotangent.astype(jnp.float32) * gain
    inv_rms = lax.rsqrt(jnp.mean(hidden_f * hidden_f, axis=-1, keepdims=True) + 1e-06)
    mixed = jnp.mean(hidden_f * scaled_cot, axis=-1, keepdims=True)
    return (inv_rms * scaled_cot - hidden_f * inv_rms * inv_rms * inv_rms * mixed).astype(
        jnp.bfloat16
    )


def upsample(handed):
    half_width = GW // 2
    grid_rows = handed.reshape(handed.shape[0] // half_width, half_width, handed.shape[1])
    grid_rows = jnp.repeat(jnp.repeat(grid_rows, 2, axis=0), 2, axis=1)
    return grid_rows.reshape(-1, handed.shape[1])


def attend_back(query_rows, key_rows, value_rows, grad_rows):
    seq_length = query_rows.shape[0]
    block_rows = min(512, seq_length)
    score_scale = query_rows.shape[1] ** (-0.5)

    def step(carry, block_index):
        grad_key, grad_value = carry
        first_row = block_index * block_rows
        query_block = lax.dynamic_slice_in_dim(query_rows, first_row, block_rows, 0)
        grad_block = lax.dynamic_slice_in_dim(grad_rows, first_row, block_rows, 0)
        scores = jnp.dot(query_block, key_rows.T, preferred_element_type=jnp.float32) * score_scale
        row_max = jnp.max(scores, axis=1, keepdims=True)
        exp_scores = jnp.exp(scores - row_max)
        attn_weights = exp_scores / jnp.sum(exp_scores, axis=1, keepdims=True)
        weights_half = attn_weights.astype(jnp.bfloat16)
        grad_weights = jnp.dot(grad_block, value_rows.T, preferred_element_type=jnp.float32)
        row_dot = jnp.sum(attn_weights * grad_weights, axis=1, keepdims=True)
        grad_scores = (attn_weights * (grad_weights - row_dot)).astype(jnp.bfloat16)
        grad_query = (
            jnp.dot(grad_scores, key_rows, preferred_element_type=jnp.float32) * score_scale
        ).astype(jnp.bfloat16)
        grad_key = grad_key + jnp.dot(
            grad_scores.T, query_block, preferred_element_type=jnp.float32
        )
        grad_value = grad_value + jnp.dot(
            weights_half.T, grad_block, preferred_element_type=jnp.float32
        )
        return ((grad_key, grad_value), grad_query)

    zeros_init = jnp.zeros(query_rows.shape, jnp.float32)
    carry, query_blocks = lax.scan(
        step, (zeros_init, zeros_init), jnp.arange(seq_length // block_rows, dtype=jnp.int32)
    )
    grad_query = query_blocks.reshape(seq_length, -1)
    grad_key = (carry[0] * score_scale).astype(jnp.bfloat16)
    grad_value = carry[1].astype(jnp.bfloat16)
    return (grad_query, grad_key, grad_value)


def heads_backward(query_rows, key_rows, value_rows, grad_rows):
    seq_length = query_rows.shape[0]
    head_count = query_rows.shape[1] // HD

    def split_heads(array):
        return array.reshape(seq_length, head_count, HD).transpose(1, 0, 2)

    def per_head(head_items):
        return attend_back(head_items[0], head_items[1], head_items[2], head_items[3])

    head_grads = lax.map(
        per_head,
        (
            split_heads(query_rows),
            split_heads(key_rows),
            split_heads(value_rows),
            split_heads(grad_rows),
        ),
    )
    return tuple(
        (grads.transpose(1, 0, 2).reshape(seq_length, head_count * HD) for grads in head_grads)
    )


def local(
    rm_hidden, rm_cotangent, rm_gain, rewards, visual_pos, bridge, img_query, img_key, img_value
):
    reward_sum = lax.psum(jnp.sum(rewards), "dp")
    sample_count = lax.axis_size("dp") * rewards.shape[0]
    reward_weight = rewards[0] * sample_count / reward_sum
    row_offset = lax.axis_index("tensor") * rm_hidden.shape[1]
    local_rows = visual_pos[0] - row_offset
    vis_hidden = jnp.take(rm_hidden[0], local_rows, axis=0)
    vis_cot = jnp.take(rm_cotangent[0], local_rows, axis=0)
    visual_grad = norm_backward(vis_hidden, vis_cot, rm_gain)
    handed = (
        jnp.dot(
            lax.all_gather(visual_grad, "tensor", axis=0, tiled=True),
            bridge,
            preferred_element_type=jnp.float32,
        )
        * reward_weight
    ).astype(jnp.bfloat16)
    grad_rows = upsample(handed)
    head_query, head_key, head_value = (
        lax.all_to_all(img_query[0], "tensor", split_axis=1, concat_axis=0, tiled=True),
        lax.all_to_all(img_key[0], "tensor", split_axis=1, concat_axis=0, tiled=True),
        lax.all_to_all(img_value[0], "tensor", split_axis=1, concat_axis=0, tiled=True),
    )
    head_grads = heads_backward(head_query, head_key, head_value, grad_rows)
    token_query, token_key, token_value = (
        lax.all_to_all(head_grads[0], "tensor", split_axis=0, concat_axis=1, tiled=True),
        lax.all_to_all(head_grads[1], "tensor", split_axis=0, concat_axis=1, tiled=True),
        lax.all_to_all(head_grads[2], "tensor", split_axis=0, concat_axis=1, tiled=True),
    )
    return (token_query[None], token_key[None], token_value[None])


def solution(mesh):
    placed = (
        P("dp", "tensor", None),
        P("dp", "tensor", None),
        P(),
        P("dp"),
        P("dp", "tensor"),
        P(None, "tensor"),
        P("dp", "tensor", None),
        P("dp", "tensor", None),
        P("dp", "tensor", None),
    )
    return jax.shard_map(
        local,
        mesh=mesh,
        in_specs=placed,
        out_specs=(P("dp", "tensor", None), P("dp", "tensor", None), P("dp", "tensor", None)),
        check_vma=False,
    )
```

profile of v0, /device:TPU:2, one launch (start us, length us, event | category | flops | bytes accessed | tf_op | source)
XLA Modules:
  0.0 156.4 jit_solution(5325367002185193584)
XLA Ops:
  0.7 1.5 all_to_all.72
  3.0 4.9 %all-to-all-start = ((bf16[128,4,512]{2,0,1:T(8,128)(2,1)}), bf16[128,4,512]{2,0,1:T(8,128)(2,1)S(1)}, u32[]{:S(2)}, u32[]{:S(2)}) async-start(bf16[128,4,512]{2,0,1:T(8,128)(2,1)} %copy.22), calls=%async_computation | async-start | bytes 1048576 | tf_op jit(solution)/shard_map/all_to_all | solution.py:111
  7.9 1.5 all_to_all.75
  10.3 12.1 %all-to-all-done = bf16[128,4,512]{2,0,1:T(8,128)(2,1)S(1)} async-done(((bf16[128,4,512]{2,0,1:T(8,128)(2,1)}), bf16[128,4,512]{2,0,1:T(8,128)(2,1)S(1)}, u32[]{:S(2)}, u32[]{:S(2)}) %all-to-all-start) | async-done | bytes 524320 | tf_op jit(solution)/shard_map/all_to_all | solution.py:111
  22.4 3.5 %all-to-all-start.1 = ((bf16[128,4,512]{2,0,1:T(8,128)(2,1)}), bf16[128,4,512]{2,0,1:T(8,128)(2,1)S(1)}, u32[]{:S(2)}, u32[]{:S(2)}) async-start(bf16[128,4,512]{2,0,1:T(8,128)(2,1)} %copy.23), calls=%async_computation.1 | async-start | bytes 1048576 | tf_op jit(solution)/shard_map/all_to_all | solution.py:112
  29.0 10.9 %all-to-all-done.1 = bf16[128,4,512]{2,0,1:T(8,128)(2,1)S(1)} async-done(((bf16[128,4,512]{2,0,1:T(8,128)(2,1)}), bf16[128,4,512]{2,0,1:T(8,128)(2,1)S(1)}, u32[]{:S(2)}, u32[]{:S(2)}) %all-to-all-start.1) | async-done | bytes 524320 | tf_op jit(solution)/shard_map/all_to_all | solution.py:112
  39.9 3.5 %all-to-all-start.2 = ((bf16[128,4,512]{2,0,1:T(8,128)(2,1)}), bf16[128,4,512]{2,0,1:T(8,128)(2,1)S(1)}, u32[]{:S(2)}, u32[]{:S(2)}) async-start(bf16[128,4,512]{2,0,1:T(8,128)(2,1)} %copy.24), calls=%async_computation.2 | async-start | bytes 1048576 | tf_op jit(solution)/shard_map/all_to_all | solution.py:113
  44.3 11.3 %psum.7 = f32[]{:T(128)} all-reduce(f32[]{:T(128)} %bitcast.14), channel_id=1, replica_groups=mesh['dp'=8,'tensor'=4] {'dp'}, use_global_device_ids=true, to_apply=%region_2.0 | all-reduce | flops 1 | bytes 8 | tf_op jit(solution)/shard_map/psum | solution.py:93
  56.9 21.2 %all_gather.3 = bf16[128,3584]{1,0:T(8,128)(2,1)S(1)} all-gather(bf16[32,3584]{1,0:T(8,128)(2,1)S(1)} %fusion.38), channel_id=1, replica_groups=mesh['dp'=8,'tensor'=4] {'tensor'}, dimensions={0}, use_global_device_ids=true | all-gather | bytes 1146880 | tf_op jit(solution)/shard_map/all_gather | solution.py:103
  78.1 2.7 %fusion.32 = bf16[128,512]{1,0:T(8,128)(2,1)S(1)} fusion(bf16[128,3584]{1,0:T(8,128)(2,1)S(1)} %all_gather.3, bf16[3584,512]{1,0:T(8,128)(2,1)} %param.18, f32[]{:T(128)S(6)} %div.23), kind=kOutput, calls=%fused_computation.41 | convolution fusion | flops 469893120 | bytes 4718596 | tf_op jit(solution)/shard_map/dot_general | solution.py:102
  83.4 16.3 %while.14 = (s32[]{:T(128)}, bf16[4,512,128]{2,1,0:T(8,128)(2,1)}, bf16[4,512,128]{2,1,0:T(8,128)(2,1)}, bf16[4,512,128]{2,1,0:T(8,128)(2,1)}, bf16[4,512,128]{2...) while((s32[]{:T(128)}, bf16[4,512,128]{2,1,0:T(8,128)(2,1)}, ...), condition=%wide.region_7.9_spmd, body=%wide.region_3.8_spmd.sunk | while | flops 340064768 | bytes 10251357 | solution.py:76
  86.5 1.0 fusion.64
  88.0 1.0 fusion.66
  90.5 1.0 fusion.64
  92.1 1.0 fusion.66
  94.6 1.0 fusion.64
  96.1 1.0 fusion.66
  98.7 1.0 fusion.64
  99.7 1.5 copy.29
  101.2 1.0 all_to_all.81
  102.2 3.8 %all-to-all-start.3 = ((bf16[4,128,512]{2,1,0:T(8,128)(2,1)}), bf16[4,128,512]{2,1,0:T(8,128)(2,1)S(1)}, u32[]{:S(2)}, u32[]{:S(2)}) async-start(bf16[4,128,512]{2,1,0:T(8,128)(2,1)} %all_to_all.81), calls=%async_computation.3 | async-start | bytes 1048576 | tf_op jit(solution)/shard_map/all_to_all | solution.py:117
  106.1 1.4 copy.31
  107.5 1.0 all_to_all.84
  108.5 11.6 %all-to-all-done.3 = bf16[4,128,512]{2,1,0:T(8,128)(2,1)S(1)} async-done(((bf16[4,128,512]{2,1,0:T(8,128)(2,1)}), bf16[4,128,512]{2,1,0:T(8,128)(2,1)S(1)}, u32[]{:S(2)}, u32[]{:S(2)}) %all-to-all-start.3) | async-done | bytes 524320 | tf_op jit(solution)/shard_map/all_to_all | solution.py:117
  120.1 3.5 %all-to-all-start.4 = ((bf16[4,128,512]{2,1,0:T(8,128)(2,1)}), bf16[4,128,512]{2,1,0:T(8,128)(2,1)S(1)}, u32[]{:S(2)}, u32[]{:S(2)}) async-start(bf16[4,128,512]{2,1,0:T(8,128)(2,1)} %all_to_all.84), calls=%async_computation.4 | async-start | bytes 1048576 | tf_op jit(solution)/shard_map/all_to_all | solution.py:118
  124.0 1.0 all_to_all.87
  125.0 12.6 %all-to-all-done.4 = bf16[4,128,512]{2,1,0:T(8,128)(2,1)S(1)} async-done(((bf16[4,128,512]{2,1,0:T(8,128)(2,1)}), bf16[4,128,512]{2,1,0:T(8,128)(2,1)S(1)}, u32[]{:S(2)}, u32[]{:S(2)}) %all-to-all-start.4) | async-done | bytes 524320 | tf_op jit(solution)/shard_map/all_to_all | solution.py:118
  137.6 3.5 %all-to-all-start.5 = ((bf16[4,128,512]{2,1,0:T(8,128)(2,1)}), bf16[4,128,512]{2,1,0:T(8,128)(2,1)S(1)}, u32[]{:S(2)}, u32[]{:S(2)}) async-start(bf16[4,128,512]{2,1,0:T(8,128)(2,1)} %all_to_all.87), calls=%async_computation.5 | async-start | bytes 1048576 | tf_op jit(solution)/shard_map/all_to_all | solution.py:119
  141.4 1.0 copy.35
  142.6 1.0 copy.36
  143.7 11.4 %all-to-all-done.5 = bf16[4,128,512]{2,1,0:T(8,128)(2,1)S(1)} async-done(((bf16[4,128,512]{2,1,0:T(8,128)(2,1)}), bf16[4,128,512]{2,1,0:T(8,128)(2,1)S(1)}, u32[]{:S(2)}, u32[]{:S(2)}) %all-to-all-start.5) | async-done | bytes 524320 | tf_op jit(solution)/shard_map/all_to_all | solution.py:119
  155.4 1.0 copy.37
  (66 shorter events, 18.7 us)
Async XLA Ops:
  0.6 25.3 %copy-start = (bf16[1,64,3584]{2,1,0:T(8,128)(2,1)S(1)}, bf16[1,64,3584]{2,1,0:T(8,128)(2,1)}, u32[]{:S(2)}) copy-start(bf16[1,64,3584]{2,1,0:T(8,128)(2,1)} %param.13) | copy-start | bytes 1376260
  0.6 25.2 %copy-start.7 = (s32[1,32]{1,0:T(1,128)S(1)}, s32[1,32]{1,0:T(1,128)}, u32[]{:S(2)}) copy-start(s32[1,32]{1,0:T(1,128)} %param.17) | copy-start | bytes 388
  2.1 24.5 %copy-start.1 = (bf16[1,64,3584]{2,1,0:T(8,128)(2,1)S(1)}, bf16[1,64,3584]{2,1,0:T(8,128)(2,1)}, u32[]{:S(2)}) copy-start(bf16[1,64,3584]{2,1,0:T(8,128)(2,1)} %param.14) | copy-start | bytes 1376260
  3.0 19.4 %all-to-all-start = ((bf16[128,4,512]{2,0,1:T(8,128)(2,1)}), bf16[128,4,512]{2,0,1:T(8,128)(2,1)S(1)}, u32[]{:S(2)}, u32[]{:S(2)}) async-start(bf16[128,4,512]{2,0,1:T(8,128)(2,1)} %copy.22), calls=%async_computation | async-start | bytes 1048576 | tf_op jit(solution)/shard_map/all_to_all | solution.py:111
  7.9 19.4 %copy-start.2 = (bf16[1,128,2048]{2,1,0:T(8,128)(2,1)S(1)}, bf16[1,128,2048]{2,1,0:T(8,128)(2,1)}, u32[]{:S(2)}) copy-start(bf16[1,128,2048]{2,1,0:T(8,128)(2,1)} %param.21) | copy-start | bytes 1572868
  10.3 18.3 %copy-start.5 = (f32[3584]{0:T(1024)S(1)}, f32[3584]{0:T(1024)}, u32[]{:S(2)}) copy-start(f32[3584]{0:T(1024)} %param.15) | copy-start | bytes 43012
  22.4 17.5 %all-to-all-start.1 = ((bf16[128,4,512]{2,0,1:T(8,128)(2,1)}), bf16[128,4,512]{2,0,1:T(8,128)(2,1)S(1)}, u32[]{:S(2)}, u32[]{:S(2)}) async-start(bf16[128,4,512]{2,0,1:T(8,128)(2,1)} %copy.23), calls=%async_computation.1 | async-start | bytes 1048576 | tf_op jit(solution)/shard_map/all_to_all | solution.py:112
  25.9 14.0 %copy-start.6 = (pred[32]{0:T(512)(128)(4,1)}, pred[32]{0:T(512)(128)(4,1)S(1)}, u32[]{:S(2)}) copy-start(pred[32]{0:T(512)(128)(4,1)S(1)} %get-tuple-element.112) | copy-start | bytes 100
  39.9 42.9 %all-to-all-start.2 = ((bf16[128,4,512]{2,0,1:T(8,128)(2,1)}), bf16[128,4,512]{2,0,1:T(8,128)(2,1)S(1)}, u32[]{:S(2)}, u32[]{:S(2)}) async-start(bf16[128,4,512]{2,0,1:T(8,128)(2,1)} %copy.24), calls=%async_computation.2 | async-start | bytes 1048576 | tf_op jit(solution)/shard_map/all_to_all | solution.py:113
  82.3 1.0 copy-start.3
  99.7 23.9 %copy-start.4 = (bf16[4,512,128]{2,1,0:T(8,128)(2,1)S(1)}, bf16[4,512,128]{2,1,0:T(8,128)(2,1)}, u32[]{:S(2)}) copy-start(bf16[4,512,128]{2,1,0:T(8,128)(2,1)} %get-tuple-element.74) | copy-start | bytes 1572868
  102.2 17.9 %all-to-all-start.3 = ((bf16[4,128,512]{2,1,0:T(8,128)(2,1)}), bf16[4,128,512]{2,1,0:T(8,128)(2,1)S(1)}, u32[]{:S(2)}, u32[]{:S(2)}) async-start(bf16[4,128,512]{2,1,0:T(8,128)(2,1)} %all_to_all.81), calls=%async_computation.3 | async-start | bytes 1048576 | tf_op jit(solution)/shard_map/all_to_all | solution.py:117
  120.1 17.5 %all-to-all-start.4 = ((bf16[4,128,512]{2,1,0:T(8,128)(2,1)}), bf16[4,128,512]{2,1,0:T(8,128)(2,1)S(1)}, u32[]{:S(2)}, u32[]{:S(2)}) async-start(bf16[4,128,512]{2,1,0:T(8,128)(2,1)} %all_to_all.84), calls=%async_computation.4 | async-start | bytes 1048576 | tf_op jit(solution)/shard_map/all_to_all | solution.py:118
  137.6 17.5 %all-to-all-start.5 = ((bf16[4,128,512]{2,1,0:T(8,128)(2,1)}), bf16[4,128,512]{2,1,0:T(8,128)(2,1)S(1)}, u32[]{:S(2)}, u32[]{:S(2)}) async-start(bf16[4,128,512]{2,1,0:T(8,128)(2,1)} %all_to_all.87), calls=%async_computation.5 | async-start | bytes 1048576 | tf_op jit(solution)/shard_map/all_to_all | solution.py:119
where the time goes:
time: 157 us; the launch traced here: 156 us
  waiting for transfers between devices  58.7 us (37%)
  blocking collectives  32.5 us (21%)
  starting transfers between devices  22.6 us (14%)
  local copies, waits for them, and re-layouts  20.1 us (13%)
  matrix products  17 us (11%)
  other arithmetic  3.17 us (2%)
  between operations  2.24 us (1%)
    all_gather x1, blocking collectives, local(): lax.all_gather(visual_grad, 'tensor', axis=0, tiled=True)  21.2 us
    all_to_all x1, waiting for transfers between devices, local(): lax.all_to_all(head_grads[1], 'tensor', split_axis=0, concat_axis=1, tile...  12.6 us
    all_to_all x1, waiting for transfers between devices, local(): lax.all_to_all(img_query[0], 'tensor', split_axis=1, concat_axis=0, tiled...  12.1 us
    all_to_all x1, waiting for transfers between devices, local(): lax.all_to_all(head_grads[0], 'tensor', split_axis=0, concat_axis=1, tile...  11.6 us
    all_to_all x1, waiting for transfers between devices, local(): lax.all_to_all(head_grads[2], 'tensor', split_axis=0, concat_axis=1, tile...  11.4 us
    psum x1, blocking collectives, local(): reward_sum = lax.psum(jnp.sum(rewards), 'dp')  11.3 us
    all_to_all x1, waiting for transfers between devices, local(): lax.all_to_all(img_key[0], 'tensor', split_axis=1, concat_axis=0, tiled=T...  10.9 us
    all_to_all x1, starting transfers between devices, local(): lax.all_to_all(img_query[0], 'tensor', split_axis=1, concat_axis=0, tiled...  4.87 us
  transfers between devices with their start and end apart: 6, of which 5 were waited for; matrix products, arithmetic and copies ran while one was open for 9% of the time, Pallas kernels for 0%

commit v1 on v0

--- a/solution.py
+++ b/solution.py
@@ -114,7 +114,12 @@
     )
     head_grads = heads_backward(head_query, head_key, head_value, grad_rows)
     token_query, token_key, token_value = (
-        lax.all_to_all(head_grads[0], "tensor", split_axis=0, concat_axis=1, tiled=True),
+        jnp.concatenate(
+            lax.all_to_all(
+                jnp.stack(jnp.split(head_grads[0], lax.axis_size("tensor"), axis=0)), "tensor", 0, 0
+            ),
+            axis=1,
+        ),
         lax.all_to_all(head_grads[1], "tensor", split_axis=0, concat_axis=1, tiled=True),
         lax.all_to_all(head_grads[2], "tensor", split_axis=0, concat_axis=1, tiled=True),
     )

time: 157 us -> 161 us (1.025)
  local copies, waits for them, and re-layouts: 20.1 us -> 22 us
    dot_general x4, matrix products: 1.31 us -> 4.91 us  [step(): jnp.dot(grad_block, value_rows.T, preferred_element_type=jnp.float32)]
    dynamic_update_slice x0 -> x8, local copies, waits for them, and re-layouts: none -> 3.14 us  [heads_backward(): lax.map(per_head, (split_heads(query_rows), split_heads(key_rows), split_...]
    dot_general x4, matrix products: 4.04 us -> 1.4 us  [step(): jnp.dot(grad_scores, key_rows, preferred_element_type=jnp.float32)]
    transpose x3 -> x2, local copies, waits for them, and re-layouts: 3.36 us -> 1.86 us  [heads_backward(): grads.transpose(1, 0, 2).reshape(seq_length, head_count * HD)]
  transfers between devices with their start and end apart: 6 -> 6, of which waited for: 5 -> 5; matrix products, arithmetic and copies ran while one was open for 9% -> 8% of each run, Pallas kernels for 0% -> 0%
where the time goes in v1:
time: 161 us; the launch traced here: 160 us
  waiting for transfers between devices  59 us (37%)
  blocking collectives  32.5 us (20%)
  starting transfers between devices  22.6 us (14%)
  local copies, waits for them, and re-layouts  22 us (14%)
  matrix products  18 us (11%)
  other arithmetic  4.04 us (3%)
  between operations  2.25 us (1%)
    all_gather x1, blocking collectives, local(): lax.all_gather(visual_grad, 'tensor', axis=0, tiled=True)  21.2 us
    all_to_all x1, waiting for transfers between devices, local(): lax.all_to_all(head_grads[1], 'tensor', split_axis=0, concat_axis=1, tile...  12.6 us
    all_to_all x1, waiting for transfers between devices, local(): lax.all_to_all(img_query[0], 'tensor', split_axis=1, concat_axis=0, tiled...  12.1 us
    all_to_all x1, waiting for transfers between devices, local(): lax.all_to_all(head_grads[2], 'tensor', split_axis=0, concat_axis=1, tile...  11.7 us
    all_to_all x1, waiting for transfers between devices, local(): lax.all_to_all(jnp.stack(jnp.split(head_grads[0], lax.axis_size('tensor')...  11.6 us
    psum x1, blocking collectives, local(): reward_sum = lax.psum(jnp.sum(rewards), 'dp')  11.3 us
    all_to_all x1, waiting for transfers between devices, local(): lax.all_to_all(img_key[0], 'tensor', split_axis=1, concat_axis=0, tiled=T...  10.9 us
    dot_general x4, matrix products, step(): jnp.dot(grad_block, value_rows.T, preferred_element_type=jnp.float32)  4.91 us
  transfers between devices with their start and end apart: 6, of which 5 were waited for; matrix products, arithmetic and copies ran while one was open for 8% of the time, Pallas kernels for 0%

profile of v1, /device:TPU:2, one launch (start us, length us, event | category | flops | bytes accessed | tf_op | source)
XLA Modules:
  0.0 160.5 jit_solution(3399656943508742722)
XLA Ops:
  0.7 1.5 all_to_all.63
  3.0 4.9 %all-to-all-start = ((bf16[128,4,512]{2,0,1:T(8,128)(2,1)}), bf16[128,4,512]{2,0,1:T(8,128)(2,1)S(1)}, u32[]{:S(2)}, u32[]{:S(2)}) async-start(bf16[128,4,512]{2,0,1:T(8,128)(2,1)} %copy.23), calls=%async_computation | async-start | bytes 1048576 | tf_op jit(solution)/shard_map/all_to_all | solution.py:111
  7.9 1.5 all_to_all.66
  10.3 12.1 %all-to-all-done = bf16[128,4,512]{2,0,1:T(8,128)(2,1)S(1)} async-done(((bf16[128,4,512]{2,0,1:T(8,128)(2,1)}), bf16[128,4,512]{2,0,1:T(8,128)(2,1)S(1)}, u32[]{:S(2)}, u32[]{:S(2)}) %all-to-all-start) | async-done | bytes 524320 | tf_op jit(solution)/shard_map/all_to_all | solution.py:111
  22.4 3.5 %all-to-all-start.1 = ((bf16[128,4,512]{2,0,1:T(8,128)(2,1)}), bf16[128,4,512]{2,0,1:T(8,128)(2,1)S(1)}, u32[]{:S(2)}, u32[]{:S(2)}) async-start(bf16[128,4,512]{2,0,1:T(8,128)(2,1)} %copy.24), calls=%async_computation.1 | async-start | bytes 1048576 | tf_op jit(solution)/shard_map/all_to_all | solution.py:112
  29.0 10.9 %all-to-all-done.1 = bf16[128,4,512]{2,0,1:T(8,128)(2,1)S(1)} async-done(((bf16[128,4,512]{2,0,1:T(8,128)(2,1)}), bf16[128,4,512]{2,0,1:T(8,128)(2,1)S(1)}, u32[]{:S(2)}, u32[]{:S(2)}) %all-to-all-start.1) | async-done | bytes 524320 | tf_op jit(solution)/shard_map/all_to_all | solution.py:112
  39.9 3.5 %all-to-all-start.2 = ((bf16[128,4,512]{2,0,1:T(8,128)(2,1)}), bf16[128,4,512]{2,0,1:T(8,128)(2,1)S(1)}, u32[]{:S(2)}, u32[]{:S(2)}) async-start(bf16[128,4,512]{2,0,1:T(8,128)(2,1)} %copy.25), calls=%async_computation.2 | async-start | bytes 1048576 | tf_op jit(solution)/shard_map/all_to_all | solution.py:113
  44.3 11.3 %psum.7 = f32[]{:T(128)} all-reduce(f32[]{:T(128)} %bitcast.14), channel_id=1, replica_groups=mesh['dp'=8,'tensor'=4] {'dp'}, use_global_device_ids=true, to_apply=%region_2.0 | all-reduce | flops 1 | bytes 8 | tf_op jit(solution)/shard_map/psum | solution.py:93
  56.9 21.2 %all_gather.3 = bf16[128,3584]{1,0:T(8,128)(2,1)S(1)} all-gather(bf16[32,3584]{1,0:T(8,128)(2,1)S(1)} %fusion.37), channel_id=1, replica_groups=mesh['dp'=8,'tensor'=4] {'tensor'}, dimensions={0}, use_global_device_ids=true | all-gather | bytes 1146880 | tf_op jit(solution)/shard_map/all_gather | solution.py:103
  78.1 2.7 %fusion.31 = bf16[128,512]{1,0:T(8,128)(2,1)S(1)} fusion(bf16[128,3584]{1,0:T(8,128)(2,1)S(1)} %all_gather.3, bf16[3584,512]{1,0:T(8,128)(2,1)} %param.18, f32[]{:T(128)S(6)} %div.23), kind=kOutput, calls=%fused_computation.41 | convolution fusion | flops 469893120 | bytes 4718596 | tf_op jit(solution)/shard_map/dot_general | solution.py:102
  83.7 20.4 %while.14 = (s32[]{:T(128)}, bf16[4,512,128]{1,2,0:T(8,128)(2,1)}, bf16[4,512,128]{2,1,0:T(8,128)(2,1)}, bf16[4,512,128]{2,1,0:T(8,128)(2,1)}, bf16[4,512,128]{2...) while((s32[]{:T(128)}, bf16[4,512,128]{1,2,0:T(8,128)(2,1)}, ...), condition=%wide.region_7.9_spmd, body=%wide.region_3.8_spmd.sunk | while | flops 340064768 | bytes 10775137 | solution.py:76
  84.2 1.0 fusion.66
  85.2 1.2 multiply_reduce_fusion.2
  89.4 1.0 fusion.66
  90.4 1.2 multiply_reduce_fusion.2
  94.5 1.0 fusion.66
  95.5 1.2 multiply_reduce_fusion.2
  99.6 1.0 fusion.66
  100.6 1.2 multiply_reduce_fusion.2
  104.2 1.2 fusion.40
  106.3 3.9 %all-to-all-start.3 = ((bf16[4,128,512]{1,2,0:T(8,128)(2,1)}), bf16[4,128,512]{1,2,0:T(8,128)(2,1)S(1)}, u32[]{:S(2)}, u32[]{:S(2)}) async-start(bf16[4,128,512]{1,2,0:T(8,128)(2,1)} %pad_maximum_fusion), calls=%async_computation.3 | async-start | bytes 1048576 | tf_op jit(solution)/shard_map/all_to_all | solution.py:118
  110.1 1.4 copy.31
  111.6 1.0 all_to_all.73
  112.6 11.6 %all-to-all-done.3 = bf16[4,128,512]{1,2,0:T(8,128)(2,1)S(1)} async-done(((bf16[4,128,512]{1,2,0:T(8,128)(2,1)}), bf16[4,128,512]{1,2,0:T(8,128)(2,1)S(1)}, u32[]{:S(2)}, u32[]{:S(2)}) %all-to-all-start.3) | async-done | bytes 524320 | tf_op jit(solution)/shard_map/all_to_all | solution.py:118
  124.2 3.5 %all-to-all-start.4 = ((bf16[4,128,512]{2,1,0:T(8,128)(2,1)}), bf16[4,128,512]{2,1,0:T(8,128)(2,1)S(1)}, u32[]{:S(2)}, u32[]{:S(2)}) async-start(bf16[4,128,512]{2,1,0:T(8,128)(2,1)} %all_to_all.73), calls=%async_computation.4 | async-start | bytes 1048576 | tf_op jit(solution)/shard_map/all_to_all | solution.py:123
  128.1 1.0 all_to_all.76
  129.1 12.6 %all-to-all-done.4 = bf16[4,128,512]{2,1,0:T(8,128)(2,1)S(1)} async-done(((bf16[4,128,512]{2,1,0:T(8,128)(2,1)}), bf16[4,128,512]{2,1,0:T(8,128)(2,1)S(1)}, u32[]{:S(2)}, u32[]{:S(2)}) %all-to-all-start.4) | async-done | bytes 524320 | tf_op jit(solution)/shard_map/all_to_all | solution.py:123
  141.7 3.5 %all-to-all-start.5 = ((bf16[4,128,512]{2,1,0:T(8,128)(2,1)}), bf16[4,128,512]{2,1,0:T(8,128)(2,1)S(1)}, u32[]{:S(2)}, u32[]{:S(2)}) async-start(bf16[4,128,512]{2,1,0:T(8,128)(2,1)} %all_to_all.76), calls=%async_computation.5 | async-start | bytes 1048576 | tf_op jit(solution)/shard_map/all_to_all | solution.py:124
  145.2 1.0 copy.35
  146.4 1.0 copy.36
  147.4 11.7 %all-to-all-done.5 = bf16[4,128,512]{2,1,0:T(8,128)(2,1)S(1)} async-done(((bf16[4,128,512]{2,1,0:T(8,128)(2,1)}), bf16[4,128,512]{2,1,0:T(8,128)(2,1)S(1)}, u32[]{:S(2)}, u32[]{:S(2)}) %all-to-all-start.5) | async-done | bytes 524320 | tf_op jit(solution)/shard_map/all_to_all | solution.py:124
  159.4 1.0 copy.37
  (73 shorter events, 21.9 us)
Async XLA Ops:
  0.6 25.3 %copy-start = (bf16[1,64,3584]{2,1,0:T(8,128)(2,1)S(1)}, bf16[1,64,3584]{2,1,0:T(8,128)(2,1)}, u32[]{:S(2)}) copy-start(bf16[1,64,3584]{2,1,0:T(8,128)(2,1)} %param.13) | copy-start | bytes 1376260
  0.6 25.2 %copy-start.7 = (s32[1,32]{1,0:T(1,128)S(1)}, s32[1,32]{1,0:T(1,128)}, u32[]{:S(2)}) copy-start(s32[1,32]{1,0:T(1,128)} %param.17) | copy-start | bytes 388
  2.1 24.5 %copy-start.1 = (bf16[1,64,3584]{2,1,0:T(8,128)(2,1)S(1)}, bf16[1,64,3584]{2,1,0:T(8,128)(2,1)}, u32[]{:S(2)}) copy-start(bf16[1,64,3584]{2,1,0:T(8,128)(2,1)} %param.14) | copy-start | bytes 1376260
  3.0 19.4 %all-to-all-start = ((bf16[128,4,512]{2,0,1:T(8,128)(2,1)}), bf16[128,4,512]{2,0,1:T(8,128)(2,1)S(1)}, u32[]{:S(2)}, u32[]{:S(2)}) async-start(bf16[128,4,512]{2,0,1:T(8,128)(2,1)} %copy.23), calls=%async_computation | async-start | bytes 1048576 | tf_op jit(solution)/shard_map/all_to_all | solution.py:111
  7.9 19.4 %copy-start.2 = (bf16[1,128,2048]{2,1,0:T(8,128)(2,1)S(1)}, bf16[1,128,2048]{2,1,0:T(8,128)(2,1)}, u32[]{:S(2)}) copy-start(bf16[1,128,2048]{2,1,0:T(8,128)(2,1)} %param.21) | copy-start | bytes 1572868
  10.3 18.3 %copy-start.5 = (f32[3584]{0:T(1024)S(1)}, f32[3584]{0:T(1024)}, u32[]{:S(2)}) copy-start(f32[3584]{0:T(1024)} %param.15) | copy-start | bytes 43012
  22.4 17.5 %all-to-all-start.1 = ((bf16[128,4,512]{2,0,1:T(8,128)(2,1)}), bf16[128,4,512]{2,0,1:T(8,128)(2,1)S(1)}, u32[]{:S(2)}, u32[]{:S(2)}) async-start(bf16[128,4,512]{2,0,1:T(8,128)(2,1)} %copy.24), calls=%async_computation.1 | async-start | bytes 1048576 | tf_op jit(solution)/shard_map/all_to_all | solution.py:112
  25.9 14.0 %copy-start.6 = (pred[32]{0:T(512)(128)(4,1)}, pred[32]{0:T(512)(128)(4,1)S(1)}, u32[]{:S(2)}) copy-start(pred[32]{0:T(512)(128)(4,1)S(1)} %get-tuple-element.115) | copy-start | bytes 100
  39.9 42.8 %all-to-all-start.2 = ((bf16[128,4,512]{2,0,1:T(8,128)(2,1)}), bf16[128,4,512]{2,0,1:T(8,128)(2,1)S(1)}, u32[]{:S(2)}, u32[]{:S(2)}) async-start(bf16[128,4,512]{2,0,1:T(8,128)(2,1)} %copy.25), calls=%async_computation.2 | async-start | bytes 1048576 | tf_op jit(solution)/shard_map/all_to_all | solution.py:113
  82.3 1.4 copy-start.3
  104.2 23.5 %copy-start.4 = (bf16[4,512,128]{2,1,0:T(8,128)(2,1)S(1)}, bf16[4,512,128]{2,1,0:T(8,128)(2,1)}, u32[]{:S(2)}) copy-start(bf16[4,512,128]{2,1,0:T(8,128)(2,1)} %get-tuple-element.74) | copy-start | bytes 1572868
  106.3 17.9 %all-to-all-start.3 = ((bf16[4,128,512]{1,2,0:T(8,128)(2,1)}), bf16[4,128,512]{1,2,0:T(8,128)(2,1)S(1)}, u32[]{:S(2)}, u32[]{:S(2)}) async-start(bf16[4,128,512]{1,2,0:T(8,128)(2,1)} %pad_maximum_fusion), calls=%async_computation.3 | async-start | bytes 1048576 | tf_op jit(solution)/shard_map/all_to_all | solution.py:118
  124.2 17.5 %all-to-all-start.4 = ((bf16[4,128,512]{2,1,0:T(8,128)(2,1)}), bf16[4,128,512]{2,1,0:T(8,128)(2,1)S(1)}, u32[]{:S(2)}, u32[]{:S(2)}) async-start(bf16[4,128,512]{2,1,0:T(8,128)(2,1)} %all_to_all.73), calls=%async_computation.4 | async-start | bytes 1048576 | tf_op jit(solution)/shard_map/all_to_all | solution.py:123
  141.7 17.5 %all-to-all-start.5 = ((bf16[4,128,512]{2,1,0:T(8,128)(2,1)}), bf16[4,128,512]{2,1,0:T(8,128)(2,1)S(1)}, u32[]{:S(2)}, u32[]{:S(2)}) async-start(bf16[4,128,512]{2,1,0:T(8,128)(2,1)} %all_to_all.76), calls=%async_computation.5 | async-start | bytes 1048576 | tf_op jit(solution)/shard_map/all_to_all | solution.py:124
